TPU v7x, 512 devices: a whole 4x8x8 slice. The times are simulated.
512 devices in a mesh: seq: 64 (over y, z), chan: 8 (over x, core).
Axes of the slice: x: 4, y: 8, z: 8, core: 2. Of those that a mesh axis runs over, the one named last changes fastest.
Arguments:
- signal_in: bfloat16 [16384, 2048], P('seq', 'chan'), may hold values from -6 to 6
- value_in: bfloat16 [16384, 2048], P('seq', 'chan'), may hold values from -6 to 6
- gate_in: bfloat16 [16384, 2048], P('seq', 'chan'), may hold values from -6 to 6
- filter_taps: bfloat16 [16384, 2048], P('seq', 'chan'), may hold values from -0.046875 to 0.046875
- skip_gain: float32 [2048], P('chan'), may hold values from -1 to 1
- turn_starts: int32 [32], replicated, may hold values from 0 to 15999, as said below
- out_weight: bfloat16 [2048, 2048], P(None, 'chan'), may hold values from -0.125 to 0.125
Outputs:
- projected: bfloat16 [16384, 2048], P('seq', 'chan')
Inputs may be any that keep to these rules, and one draw needn't show every extreme that they name: `turn_starts`: strictly rising; the first is 0; for k from 1 the k-th lies in [k * 512 - 512 // 4, k * 512 + 512 // 4); the last is (31) * 512 + 512 // 4 - 1.
All inputs are finite; a program needn't handle non-finite values.
Results may differ from a plain program's by a relative error of at most 0.0057.
Values may be sent and summed in bfloat16 or wider, within the bound.
A program may use at most 64 MiB of HBM per device.

v0:
```python
import functools
import math

import jax
import jax.numpy as jnp
import ml_dtypes
import numpy as np
from jax import lax
from jax.experimental import pallas as pl
from jax.experimental.pallas import tpu as pltpu
from jax.sharding import PartitionSpec as P

MESH = pl.DeviceIdType.MESH
F32 = jnp.float32
BF16 = jnp.bfloat16


def split_table(table):
    high = table.astype(ml_dtypes.bfloat16)
    low = (table - high.astype(np.float64)).astype(ml_dtypes.bfloat16)
    return high, low


def make_tables(groups, rows):
    length = 2 * groups * rows
    outer = np.arange(groups)
    inner = np.arange(rows)
    odd = 2 * outer + 1
    angle = 2.0 * math.pi * (odd[:, None] * outer[None, :] % (4 * groups)) / (4 * groups)
    first = np.concatenate([np.cos(angle), -np.sin(angle)], axis=0)
    twist = 2.0 * math.pi * (odd[:, None] * inner[None, :] % (2 * length)) / (2 * length)
    angle = 2.0 * math.pi * (inner[:, None] * inner[None, :] % rows) / rows
    cos, sin = np.cos(angle), np.sin(angle)
    middle = np.block([[cos, -sin], [sin, cos]])
    last = first.T * (2.0 / length)
    return (
        *split_table(first),
        *split_table(last),
        *split_table(middle),
        np.cos(twist).astype(np.float32),
        np.sin(twist).astype(np.float32),
    )


def halves(value):
    high = value.astype(BF16)
    return high, (value - high.astype(F32)).astype(BF16)


def dot(left, right, dims=((1,), (0,))):
    return lax.dot_general(left, right, (dims, ((), ())), preferred_element_type=F32)


def kernel(
    groups,
    chans,
    signal_ref,
    value_ref,
    gate_ref,
    taps_ref,
    skip_ref,
    starts_ref,
    weight_ref,
    first_hi_ref,
    first_lo_ref,
    last_hi_ref,
    last_lo_ref,
    mid_hi_ref,
    mid_lo_ref,
    twist_cos_ref,
    twist_sin_ref,
    out_ref,
    out_bf,
    in_bf,
    in_f32,
    spec_hi,
    spec_lo,
    back_f32,
    back_bf,
    home_bf,
    gated_all,
    weight_all,
    send_sem,
    recv_sem,
    back_send_sem,
    back_recv_sem,
    weight_send_sem,
    weight_recv_sem,
    gated_send_sem,
    gated_recv_sem,
):
    rows, width = signal_ref.shape
    own = width // groups
    half = rows // 2
    me = lax.axis_index("seq")
    mine = lax.axis_index("chan")
    core = lax.rem(mine, 2)
    sibling = mine + 1 - 2 * core

    barrier = pltpu.get_barrier_semaphore()

    @pl.loop(1, chans)
    def _(step):
        pl.semaphore_signal(
            barrier, inc=1, device_id={"chan": lax.rem(mine + step, chans)}, device_id_type=MESH
        )

    @pl.loop(1, groups)
    def _(step):
        pl.semaphore_signal(
            barrier, inc=1, device_id={"seq": lax.rem(me + step, groups)}, device_id_type=MESH
        )

    mixed = (signal_ref[...].astype(F32) * value_ref[...].astype(F32)).astype(BF16)
    row_id = lax.broadcasted_iota(jnp.int32, (2 * width, width), 0)
    col_id = lax.broadcasted_iota(jnp.int32, (2 * width, width), 1)
    target = 2 * own * (col_id // own) + lax.rem(col_id, own)
    pick_signal = (row_id == target).astype(F32).astype(BF16)
    pick_taps = (row_id == target + own).astype(F32).astype(BF16)
    turned = dot(pick_signal, mixed, ((1,), (1,))) + dot(pick_taps, taps_ref[...], ((1,), (1,)))
    out_bf[...] = turned.reshape(groups, 2 * own, rows).astype(BF16)

    pl.semaphore_wait(barrier, groups + chans - 2)

    @pl.loop(1, groups)
    def _(step):
        peer = lax.rem(me + step, groups)
        pltpu.make_async_remote_copy(
            src_ref=out_bf.at[peer],
            dst_ref=in_bf.at[me],
            send_sem=send_sem,
            recv_sem=recv_sem,
            device_id={"seq": peer},
            device_id_type=MESH,
        ).start()

    @pl.loop(1, chans)
    def _(step):
        peer = lax.rem(mine + step, chans)
        pltpu.make_async_remote_copy(
            src_ref=weight_ref.at[pl.ds(peer * width, width)],
            dst_ref=weight_all.at[mine],
            send_sem=weight_send_sem,
            recv_sem=weight_recv_sem,
            device_id={"chan": peer},
            device_id_type=MESH,
        ).start()

    in_bf[pl.ds(me, 1)] = out_bf[pl.ds(me, 1)]
    weight_all[pl.ds(mine, 1)] = weight_ref[pl.ds(mine * width, width)].reshape(1, width, width)
    positions = me * rows + lax.broadcasted_iota(jnp.int32, (rows, starts_ref.shape[1]), 0)
    counted = jnp.sum(
        jnp.where(starts_ref[...] <= positions, 1.0, 0.0).astype(F32), axis=1, keepdims=True
    )
    keep = counted - 2.0 * jnp.floor(0.5 * counted)
    twist_cos = twist_cos_ref[...]
    twist_sin = twist_sin_ref[...]

    whole = in_bf.at[pl.ds(0, groups - 1)]
    pltpu.make_async_copy(whole, whole, recv_sem).wait()

    in_f32[...] = in_bf[...].astype(F32)
    for slot in range(2 * own):
        data = in_f32[:, slot, :].astype(BF16)
        raw = dot(first_hi_ref[...], data) + dot(first_lo_ref[...], data)
        real, imag = raw[:groups], raw[groups:]
        here = pl.ds(slot * groups, groups)
        spec_hi[here, :rows], spec_lo[here, :rows] = halves(real * twist_cos + imag * twist_sin)
        spec_hi[here, rows:], spec_lo[here, rows:] = halves(imag * twist_cos - real * twist_sin)
    spectrum = (
        dot(spec_hi[...], mid_hi_ref[...])
        + dot(spec_lo[...], mid_hi_ref[...])
        + dot(spec_hi[...], mid_lo_ref[...])
    )
    middle = own * groups
    z_re, z_im = spectrum[:middle, :rows], spectrum[:middle, rows:]
    h_re, h_im = spectrum[middle:, :rows], spectrum[middle:, rows:]
    prod_hi, prod_lo = halves(
        jnp.concatenate([z_re * h_re - z_im * h_im, z_re * h_im + z_im * h_re], axis=1)
    )
    inverse = (
        dot(prod_hi, mid_hi_ref[...], ((1,), (1,)))
        + dot(prod_lo, mid_hi_ref[...], ((1,), (1,)))
        + dot(prod_hi, mid_lo_ref[...], ((1,), (1,)))
    )
    for slot in range(own):
        real = inverse[slot * groups : (slot + 1) * groups, :rows]
        imag = inverse[slot * groups : (slot + 1) * groups, rows:]
        high, low = halves(
            jnp.concatenate(
                [real * twist_cos - imag * twist_sin, imag * twist_cos + real * twist_sin], axis=0
            )
        )
        result = (
            dot(last_hi_ref[...], high) + dot(last_hi_ref[...], low) + dot(last_lo_ref[...], high)
        )
        back_f32[:, 2 * slot, :] = result[:, :half]
        back_f32[:, 2 * slot + 1, :] = result[:, half:]
    back_bf[...] = back_f32[...].astype(BF16)

    @pl.loop(1, groups)
    def _(step):
        peer = lax.rem(me + step, groups)
        pltpu.make_async_remote_copy(
            src_ref=back_bf.at[peer],
            dst_ref=home_bf.at[me],
            send_sem=back_send_sem,
            recv_sem=back_recv_sem,
            device_id={"seq": peer},
            device_id_type=MESH,
        ).start()

    home_bf[pl.ds(me, 1)] = back_bf[pl.ds(me, 1)]
    direct = skip_ref[...] * mixed.astype(F32)
    scale = gate_ref[...].astype(F32) * keep
    whole = home_bf.at[pl.ds(0, groups - 1)]
    pltpu.make_async_copy(whole, whole, back_recv_sem).wait()

    home = home_bf[...].astype(F32).reshape(2 * width, half).astype(BF16)
    slot_id = lax.broadcasted_iota(jnp.int32, (2 * width, width), 0)
    chan_id = lax.broadcasted_iota(jnp.int32, (2 * width, width), 1)
    for part in range(2):
        pick = (slot_id == 2 * chan_id + part).astype(F32).astype(BF16)
        conv = dot(home, pick, ((0,), (0,)))
        span = slice(part * half, (part + 1) * half)
        gated = (scale[span] * (conv + direct[span])).astype(BF16)
        gated_all[pl.ds(mine, 1), span, :] = gated.reshape(1, half, width)

    def gated_copy(source, peer, index):
        return pltpu.make_async_remote_copy(
            src_ref=gated_all.at[source],
            dst_ref=gated_all.at[source],
            send_sem=gated_send_sem.at[index],
            recv_sem=gated_recv_sem.at[source],
            device_id={"chan": peer},
            device_id_type=MESH,
        )

    sources = [lax.rem(mine + 2 * step, chans) for step in range(1, chans // 2)]
    sends = [gated_copy(mine, peer, index) for index, peer in enumerate(sources)]
    sends.append(gated_copy(mine, sibling, len(sources)))
    for send in sends:
        send.start()

    whole = weight_all.at[pl.ds(0, chans - 1)]
    pltpu.make_async_copy(whole, whole, weight_recv_sem).wait()

    def term(source):
        return dot(gated_all[source], weight_all[source], ((1,), (1,)))

    def arrived(source):
        block = gated_all.at[source]
        pltpu.make_async_copy(block, block, gated_recv_sem.at[source]).wait()

    total = term(mine)
    order = sorted(range(len(sources)), key=lambda i: min(i + 1, len(sources) - i))
    for i in order:
        arrived(sources[i])
        forward = gated_copy(sources[i], sibling, len(sources) + 1 + i)
        forward.start()
        sends.append(forward)
        total += term(sources[i])
    arrived(sibling)
    total += term(sibling)
    for i in order:
        other = lax.rem(sources[i] + 1, 2) * 1 + (sources[i] - lax.rem(sources[i], 2))
        arrived(other)
        total += term(other)
    out_ref[...] = total.astype(BF16)

    for send in sends:
        send.wait_send()
    for block, sem, count in (
        (in_bf, send_sem, groups - 1),
        (home_bf, back_send_sem, groups - 1),
        (weight_all, weight_send_sem, chans - 1),
    ):
        whole = block.at[pl.ds(0, count)]
        pltpu.make_async_copy(whole, whole, sem).wait()


def on_device(signal_in, value_in, gate_in, filter_taps, skip_gain, turn_starts, out_weight):
    rows, width = signal_in.shape
    groups = lax.axis_size("seq")
    chans = lax.axis_size("chan")
    own = width // groups
    tables = [jnp.asarray(table) for table in make_tables(groups, rows)]
    dma = pltpu.SemaphoreType.DMA
    return pl.pallas_call(
        functools.partial(kernel, groups, chans),
        out_shape=jax.ShapeDtypeStruct((rows, width), BF16),
        in_specs=[pl.BlockSpec(memory_space=pltpu.VMEM)] * (7 + len(tables)),
        out_specs=pl.BlockSpec(memory_space=pltpu.VMEM),
        scratch_shapes=[
            pltpu.VMEM((groups, 2 * own, rows), BF16),
            pltpu.VMEM((groups, 2 * own, rows), BF16),
            pltpu.VMEM((groups, 2 * own, rows), F32),
            pltpu.VMEM((2 * own * groups, 2 * rows), BF16),
            pltpu.VMEM((2 * own * groups, 2 * rows), BF16),
            pltpu.VMEM((groups, 2 * own, rows // 2), F32),
            pltpu.VMEM((groups, 2 * own, rows // 2), BF16),
            pltpu.VMEM((groups, 2 * own, rows // 2), BF16),
            pltpu.VMEM((chans, rows, width), BF16),
            pltpu.VMEM((chans, width, width), BF16),
            dma,
            dma,
            dma,
            dma,
            dma,
            dma,
            dma((chans,)),
            dma((chans,)),
        ],
        compiler_params=pltpu.CompilerParams(collective_id=0, has_side_effects=True),
    )(
        signal_in,
        value_in,
        gate_in,
        filter_taps,
        skip_gain.reshape(1, width),
        turn_starts.reshape(1, -1),
        out_weight,
        *tables,
    )


def solution(mesh):
    in_specs = (
        P("seq", "chan"),
        P("seq", "chan"),
        P("seq", "chan"),
        P("seq", "chan"),
        P("chan"),
        P(),
        P(None, "chan"),
    )
    out_specs = P("seq", "chan")
    return jax.shard_map(
        on_device, mesh=mesh, in_specs=in_specs, out_specs=out_specs, check_vma=False
    )
```

profile of v0, /device:TPU:1, one launch (start us, length us, event | category | flops | bytes accessed | tf_op | source)
XLA Modules:
  0.0 51.2 jit_solution(15836247996027247545)
XLA Ops:
  0.0 49.6 %shard_map.145 = bf16[256,256]{1,0:T(8,128)(2,1)} custom-call(bf16[256,256]{1,0:T(8,128)(2,1)} %signal_ref.1, bf16[256,256]{1,0:T(8,128)(2,1)} %value_ref.1, bf16[256,256]{1,0:T(8,128)(2,1)} %gate_ref.1, bf16[256,256]{1,0:T(8,128)(2,1)} %taps_ref.1, f32[1,256]{1,0:T(1,128)} %bitcast.2, s32[1,32]{1,0:T(1,128)} %bitcast.3, bf16[2048,256]{1,0:T(8,128)(2,1)} %weight_ref.1, ...), custom_call_target="tpu_custom_call" | custom-call | tf_op jit(solution)/shard_map/pallas_call | solution.py:289
  49.6 1.6 %copy.17 = bf16[256,256]{1,0:T(8,128)(2,1)} copy(bf16[256,256]{1,0:T(8,128)(2,1)} %shard_map.145) | data formatting | bytes 262144
where the time goes:
time: 51.3 us; the launch traced here: 51.2 us
  Pallas kernels  49.6 us (97%)
  local copies, waits for them, and re-layouts  1.57 us (3%)
    pallas_call x1, Pallas kernels, on_device(): pl.pallas_call(functools.partial(kernel, groups, chans), out_shape=jax.Sh...  49.6 us
    unnamed x1, local copies, waits for them, and re-layouts  1.57 us

commit v1 on v0

--- a/solution.py
+++ b/solution.py
@@ -49,6 +49,10 @@
 
 def dot(left, right, dims=((1,), (0,))):
     return lax.dot_general(left, right, (dims, ((), ())), preferred_element_type=F32)
+
+
+def farthest(step, size):
+    return lax.rem(size // 2 + (1 - 2 * lax.rem(step, 2)) * ((step + 1) // 2), size)
 
 
 def kernel(
@@ -80,6 +84,12 @@
     home_bf,
     gated_all,
     weight_all,
+    passing,
+    mid_hi,
+    mid_lo,
+    load_sem,
+    first_send_sem,
+    first_recv_sem,
     send_sem,
     recv_sem,
     back_send_sem,
@@ -92,12 +102,25 @@
     rows, width = signal_ref.shape
     own = width // groups
     half = rows // 2
+    side = math.isqrt(groups)
     me = lax.axis_index("seq")
     mine = lax.axis_index("chan")
+    row, col = me // side, lax.rem(me, side)
     core = lax.rem(mine, 2)
     sibling = mine + 1 - 2 * core
 
+    def along_row(step):
+        return lax.rem(col + farthest(step, side), side)
+
+    def along_col(step):
+        return lax.rem(row + farthest(step, side), side)
+
     barrier = pltpu.get_barrier_semaphore()
+
+    @pl.loop(0, side - 1)
+    def _(step):
+        for peer in (along_col(step) * side + col, row * side + along_row(step)):
+            pl.semaphore_signal(barrier, inc=1, device_id={"seq": peer}, device_id_type=MESH)
 
     @pl.loop(1, chans)
     def _(step):
@@ -105,11 +128,15 @@
             barrier, inc=1, device_id={"chan": lax.rem(mine + step, chans)}, device_id_type=MESH
         )
 
-    @pl.loop(1, groups)
-    def _(step):
-        pl.semaphore_signal(
-            barrier, inc=1, device_id={"seq": lax.rem(me + step, groups)}, device_id_type=MESH
-        )
+    loads = [
+        pltpu.make_async_copy(mid_hi_ref, mid_hi, load_sem.at[0]),
+        pltpu.make_async_copy(mid_lo_ref, mid_lo, load_sem.at[1]),
+        pltpu.make_async_copy(
+            weight_ref.at[pl.ds(mine * width, width)], weight_all.at[mine], load_sem.at[2]
+        ),
+    ]
+    for load in loads:
+        load.start()
 
     mixed = (signal_ref[...].astype(F32) * value_ref[...].astype(F32)).astype(BF16)
     row_id = lax.broadcasted_iota(jnp.int32, (2 * width, width), 0)
@@ -118,21 +145,38 @@
     pick_signal = (row_id == target).astype(F32).astype(BF16)
     pick_taps = (row_id == target + own).astype(F32).astype(BF16)
     turned = dot(pick_signal, mixed, ((1,), (1,))) + dot(pick_taps, taps_ref[...], ((1,), (1,)))
-    out_bf[...] = turned.reshape(groups, 2 * own, rows).astype(BF16)
-
-    pl.semaphore_wait(barrier, groups + chans - 2)
-
-    @pl.loop(1, groups)
-    def _(step):
-        peer = lax.rem(me + step, groups)
+    out_bf[...] = turned.reshape(side, side, 2 * own, rows).astype(BF16)
+
+    pl.semaphore_wait(barrier, 2 * (side - 1) + chans - 1)
+
+    @pl.loop(0, side - 1)
+    def _(step):
+        peer = along_col(step)
         pltpu.make_async_remote_copy(
             src_ref=out_bf.at[peer],
-            dst_ref=in_bf.at[me],
-            send_sem=send_sem,
-            recv_sem=recv_sem,
-            device_id={"seq": peer},
+            dst_ref=passing.at[row],
+            send_sem=first_send_sem,
+            recv_sem=first_recv_sem.at[row],
+            device_id={"seq": peer * side + col},
             device_id_type=MESH,
         ).start()
+
+    def pass_on(block, source):
+        @pl.loop(0, side - 1)
+        def _(step):
+            peer = along_row(step)
+            pltpu.make_async_remote_copy(
+                src_ref=block.at[source, peer],
+                dst_ref=in_bf.at[source, col],
+                send_sem=send_sem,
+                recv_sem=recv_sem,
+                device_id={"seq": row * side + peer},
+                device_id_type=MESH,
+            ).start()
+
+        in_bf[pl.ds(source, 1), pl.ds(col, 1)] = block[pl.ds(source, 1), pl.ds(col, 1)]
+
+    pass_on(out_bf, row)
 
     @pl.loop(1, chans)
     def _(step):
@@ -146,8 +190,13 @@
             device_id_type=MESH,
         ).start()
 
-    in_bf[pl.ds(me, 1)] = out_bf[pl.ds(me, 1)]
-    weight_all[pl.ds(mine, 1)] = weight_ref[pl.ds(mine * width, width)].reshape(1, width, width)
+    @pl.loop(0, side - 1)
+    def _(step):
+        source = along_col(step)
+        block = passing.at[source]
+        pltpu.make_async_copy(block, block, first_recv_sem.at[source]).wait()
+        pass_on(passing, source)
+
     positions = me * rows + lax.broadcasted_iota(jnp.int32, (rows, starts_ref.shape[1]), 0)
     counted = jnp.sum(
         jnp.where(starts_ref[...] <= positions, 1.0, 0.0).astype(F32), axis=1, keepdims=True
@@ -156,10 +205,12 @@
     twist_cos = twist_cos_ref[...]
     twist_sin = twist_sin_ref[...]
 
-    whole = in_bf.at[pl.ds(0, groups - 1)]
+    whole = in_bf.at[pl.ds(0, side - 1)]
     pltpu.make_async_copy(whole, whole, recv_sem).wait()
-
-    in_f32[...] = in_bf[...].astype(F32)
+    for load in loads:
+        load.wait()
+
+    in_f32[...] = in_bf[...].astype(F32).reshape(groups, 2 * own, rows)
     for slot in range(2 * own):
         data = in_f32[:, slot, :].astype(BF16)
         raw = dot(first_hi_ref[...], data) + dot(first_lo_ref[...], data)
@@ -168,9 +219,9 @@
         spec_hi[here, :rows], spec_lo[here, :rows] = halves(real * twist_cos + imag * twist_sin)
         spec_hi[here, rows:], spec_lo[here, rows:] = halves(imag * twist_cos - real * twist_sin)
     spectrum = (
-        dot(spec_hi[...], mid_hi_ref[...])
-        + dot(spec_lo[...], mid_hi_ref[...])
-        + dot(spec_hi[...], mid_lo_ref[...])
+        dot(spec_hi[...], mid_hi[...])
+        + dot(spec_lo[...], mid_hi[...])
+        + dot(spec_hi[...], mid_lo[...])
     )
     middle = own * groups
     z_re, z_im = spectrum[:middle, :rows], spectrum[:middle, rows:]
@@ -179,9 +230,9 @@
         jnp.concatenate([z_re * h_re - z_im * h_im, z_re * h_im + z_im * h_re], axis=1)
     )
     inverse = (
-        dot(prod_hi, mid_hi_ref[...], ((1,), (1,)))
-        + dot(prod_lo, mid_hi_ref[...], ((1,), (1,)))
-        + dot(prod_hi, mid_lo_ref[...], ((1,), (1,)))
+        dot(prod_hi, mid_hi[...], ((1,), (1,)))
+        + dot(prod_lo, mid_hi[...], ((1,), (1,)))
+        + dot(prod_hi, mid_lo[...], ((1,), (1,)))
     )
     for slot in range(own):
         real = inverse[slot * groups : (slot + 1) * groups, :rows]
@@ -198,9 +249,9 @@
         back_f32[:, 2 * slot + 1, :] = result[:, half:]
     back_bf[...] = back_f32[...].astype(BF16)
 
-    @pl.loop(1, groups)
-    def _(step):
-        peer = lax.rem(me + step, groups)
+    @pl.loop(0, groups - 1)
+    def _(step):
+        peer = along_col(step // side) * side + along_row(lax.rem(step, side))
         pltpu.make_async_remote_copy(
             src_ref=back_bf.at[peer],
             dst_ref=home_bf.at[me],
@@ -226,21 +277,31 @@
         gated = (scale[span] * (conv + direct[span])).astype(BF16)
         gated_all[pl.ds(mine, 1), span, :] = gated.reshape(1, half, width)
 
-    def gated_copy(source, peer, index):
-        return pltpu.make_async_remote_copy(
-            src_ref=gated_all.at[source],
-            dst_ref=gated_all.at[source],
-            send_sem=gated_send_sem.at[index],
-            recv_sem=gated_recv_sem.at[source],
+    sends = []
+
+    def gated_copy(source, part, peer):
+        block = gated_all.at[source, pl.ds(part * half, half)]
+        copy = pltpu.make_async_remote_copy(
+            src_ref=block,
+            dst_ref=block,
+            send_sem=gated_send_sem.at[len(sends)],
+            recv_sem=gated_recv_sem.at[source, part],
             device_id={"chan": peer},
             device_id_type=MESH,
         )
-
-    sources = [lax.rem(mine + 2 * step, chans) for step in range(1, chans // 2)]
-    sends = [gated_copy(mine, peer, index) for index, peer in enumerate(sources)]
-    sends.append(gated_copy(mine, sibling, len(sources)))
-    for send in sends:
-        send.start()
+        copy.start()
+        sends.append(copy)
+
+    def arrived(source, part):
+        block = gated_all.at[source, pl.ds(part * half, half)]
+        pltpu.make_async_copy(block, block, gated_recv_sem.at[source, part]).wait()
+
+    right, far, left = [lax.rem(mine + 2 * step, chans) for step in (1, 2, 3)]
+    for part in range(2):
+        gated_copy(mine, part, right)
+        gated_copy(mine, 1 - part, left)
+    for part in range(2):
+        gated_copy(mine, part, sibling)
 
     whole = weight_all.at[pl.ds(0, chans - 1)]
     pltpu.make_async_copy(whole, whole, weight_recv_sem).wait()
@@ -248,30 +309,34 @@
     def term(source):
         return dot(gated_all[source], weight_all[source], ((1,), (1,)))
 
-    def arrived(source):
-        block = gated_all.at[source]
-        pltpu.make_async_copy(block, block, gated_recv_sem.at[source]).wait()
-
     total = term(mine)
-    order = sorted(range(len(sources)), key=lambda i: min(i + 1, len(sources) - i))
-    for i in order:
-        arrived(sources[i])
-        forward = gated_copy(sources[i], sibling, len(sources) + 1 + i)
-        forward.start()
-        sends.append(forward)
-        total += term(sources[i])
-    arrived(sibling)
+    for source, part, onward in ((left, 0, right), (right, 1, left)):
+        arrived(source, part)
+        gated_copy(source, part, onward)
+        gated_copy(source, part, sibling)
+    for source, part in ((left, 1), (right, 0)):
+        arrived(source, part)
+        gated_copy(source, part, sibling)
+        total += term(source)
+    arrived(sibling, 0)
+    arrived(sibling, 1)
     total += term(sibling)
-    for i in order:
-        other = lax.rem(sources[i] + 1, 2) * 1 + (sources[i] - lax.rem(sources[i], 2))
-        arrived(other)
+    for part in range(2):
+        arrived(far, part)
+        gated_copy(far, part, sibling)
+    total += term(far)
+    for source in (left, right, far):
+        other = source + 1 - 2 * core
+        arrived(other, 0)
+        arrived(other, 1)
         total += term(other)
     out_ref[...] = total.astype(BF16)
 
     for send in sends:
         send.wait_send()
     for block, sem, count in (
-        (in_bf, send_sem, groups - 1),
+        (passing, first_send_sem, side - 1),
+        (in_bf, send_sem, side - 1),
         (home_bf, back_send_sem, groups - 1),
         (weight_all, weight_send_sem, chans - 1),
     ):
@@ -284,16 +349,20 @@
     groups = lax.axis_size("seq")
     chans = lax.axis_size("chan")
     own = width // groups
+    side = math.isqrt(groups)
     tables = [jnp.asarray(table) for table in make_tables(groups, rows)]
     dma = pltpu.SemaphoreType.DMA
     return pl.pallas_call(
         functools.partial(kernel, groups, chans),
         out_shape=jax.ShapeDtypeStruct((rows, width), BF16),
-        in_specs=[pl.BlockSpec(memory_space=pltpu.VMEM)] * (7 + len(tables)),
+        in_specs=[
+            pl.BlockSpec(memory_space=pl.ANY if place in (6, 11, 12) else pltpu.VMEM)
+            for place in range(7 + len(tables))
+        ],
         out_specs=pl.BlockSpec(memory_space=pltpu.VMEM),
         scratch_shapes=[
-            pltpu.VMEM((groups, 2 * own, rows), BF16),
-            pltpu.VMEM((groups, 2 * own, rows), BF16),
+            pltpu.VMEM((side, side, 2 * own, rows), BF16),
+            pltpu.VMEM((side, side, 2 * own, rows), BF16),
             pltpu.VMEM((groups, 2 * own, rows), F32),
             pltpu.VMEM((2 * own * groups, 2 * rows), BF16),
             pltpu.VMEM((2 * own * groups, 2 * rows), BF16),
@@ -302,14 +371,20 @@
             pltpu.VMEM((groups, 2 * own, rows // 2), BF16),
             pltpu.VMEM((chans, rows, width), BF16),
             pltpu.VMEM((chans, width, width), BF16),
-            dma,
-            dma,
-            dma,
-            dma,
-            dma,
-            dma,
-            dma((chans,)),
-            dma((chans,)),
+            pltpu.VMEM((side, side, 2 * own, rows), BF16),
+            pltpu.VMEM((2 * rows, 2 * rows), BF16),
+            pltpu.VMEM((2 * rows, 2 * rows), BF16),
+            dma((3,)),
+            dma,
+            dma((side,)),
+            dma,
+            dma,
+            dma,
+            dma,
+            dma,
+            dma,
+            dma((14,)),
+            dma((chans, 2)),
         ],
         compiler_params=pltpu.CompilerParams(collective_id=0, has_side_effects=True),
     )(

time: 51.3 us -> 51.8 us (level)
    pallas_call x1, Pallas kernels: 49.6 us -> 50.1 us  [on_device(): pl.pallas_call(functools.partial(kernel, groups, chans), out_shape=jax.Sh...]
where the time goes in v1:
time: 51.8 us; the launch traced here: 51.7 us
  Pallas kernels  50.1 us (97%)
  local copies, waits for them, and re-layouts  1.57 us (3%)
    pallas_call x1, Pallas kernels, on_device(): pl.pallas_call(functools.partial(kernel, groups, chans), out_shape=jax.Sh...  50.1 us
    unnamed x1, local copies, waits for them, and re-layouts  1.57 us

profile of v1, /device:TPU:1, one launch (start us, length us, event | category | flops | bytes accessed | tf_op | source)
XLA Modules:
  0.0 51.7 jit_solution(3198602065926351273)
XLA Ops:
  0.0 50.1 %shard_map.145 = bf16[256,256]{1,0:T(8,128)(2,1)} custom-call(bf16[256,256]{1,0:T(8,128)(2,1)} %signal_ref.1, bf16[256,256]{1,0:T(8,128)(2,1)} %value_ref.1, bf16[256,256]{1,0:T(8,128)(2,1)} %gate_ref.1, bf16[256,256]{1,0:T(8,128)(2,1)} %taps_ref.1, f32[1,256]{1,0:T(1,128)} %bitcast.2, s32[1,32]{1,0:T(1,128)} %bitcast.3, bf16[2048,256]{1,0:T(8,128)(2,1)} %weight_ref.1, ...), custom_call_target="tpu_custom_call" | custom-call | tf_op jit(solution)/shard_map/pallas_call | solution.py:355
  50.1 1.6 %copy.17 = bf16[256,256]{1,0:T(8,128)(2,1)} copy(bf16[256,256]{1,0:T(8,128)(2,1)} %shard_map.145) | data formatting | bytes 262144

commit v2 on v0

--- a/solution.py
+++ b/solution.py
@@ -10,6 +10,7 @@
 from jax.experimental.pallas import tpu as pltpu
 from jax.sharding import PartitionSpec as P
 
+PIECES = 2
 MESH = pl.DeviceIdType.MESH
 F32 = jnp.float32
 BF16 = jnp.bfloat16
@@ -51,24 +52,28 @@
     return lax.dot_general(left, right, (dims, ((), ())), preferred_element_type=F32)
 
 
+def farthest(step, size):
+    return lax.rem(size // 2 + (1 - 2 * lax.rem(step, 2)) * ((step + 1) // 2), size)
+
+
 def kernel(
     groups,
     chans,
-    signal_ref,
-    value_ref,
-    gate_ref,
-    taps_ref,
-    skip_ref,
-    starts_ref,
+    signal_hbm,
+    value_hbm,
+    gate_hbm,
+    taps_hbm,
+    skip_hbm,
+    starts_hbm,
     weight_ref,
-    first_hi_ref,
-    first_lo_ref,
-    last_hi_ref,
-    last_lo_ref,
-    mid_hi_ref,
-    mid_lo_ref,
-    twist_cos_ref,
-    twist_sin_ref,
+    first_hi_hbm,
+    first_lo_hbm,
+    last_hi_hbm,
+    last_lo_hbm,
+    mid_hi_hbm,
+    mid_lo_hbm,
+    twist_cos_hbm,
+    twist_sin_hbm,
     out_ref,
     out_bf,
     in_bf,
@@ -80,6 +85,21 @@
     home_bf,
     gated_all,
     weight_all,
+    signal_ref,
+    value_ref,
+    gate_ref,
+    taps_ref,
+    skip_ref,
+    starts_ref,
+    first_hi_ref,
+    first_lo_ref,
+    last_hi_ref,
+    last_lo_ref,
+    mid_hi_ref,
+    mid_lo_ref,
+    twist_cos_ref,
+    twist_sin_ref,
+    load_sem,
     send_sem,
     recv_sem,
     back_send_sem,
@@ -89,15 +109,32 @@
     gated_send_sem,
     gated_recv_sem,
 ):
-    rows, width = signal_ref.shape
+    rows, width = signal_hbm.shape
     own = width // groups
     half = rows // 2
+    side = math.isqrt(groups)
     me = lax.axis_index("seq")
     mine = lax.axis_index("chan")
+    row, col = me // side, lax.rem(me, side)
     core = lax.rem(mine, 2)
     sibling = mine + 1 - 2 * core
 
+    def along_row(step):
+        return lax.rem(col + farthest(step, side), side)
+
+    def along_col(step):
+        return lax.rem(row + farthest(step, side), side)
+
+    def peer_of(step):
+        return along_col(step // side) * side + along_row(lax.rem(step, side))
+
     barrier = pltpu.get_barrier_semaphore()
+
+    @pl.loop(0, groups - 1)
+    def _(step):
+        pl.semaphore_signal(
+            barrier, inc=1, device_id={"seq": peer_of(step)}, device_id_type=MESH
+        )
 
     @pl.loop(1, chans)
     def _(step):
@@ -105,11 +142,35 @@
             barrier, inc=1, device_id={"chan": lax.rem(mine + step, chans)}, device_id_type=MESH
         )
 
-    @pl.loop(1, groups)
-    def _(step):
-        pl.semaphore_signal(
-            barrier, inc=1, device_id={"seq": lax.rem(me + step, groups)}, device_id_type=MESH
-        )
+    held = (
+        (signal_hbm, signal_ref),
+        (value_hbm, value_ref),
+        (gate_hbm, gate_ref),
+        (taps_hbm, taps_ref),
+        (skip_hbm, skip_ref),
+        (starts_hbm, starts_ref),
+        (first_hi_hbm, first_hi_ref),
+        (first_lo_hbm, first_lo_ref),
+        (last_hi_hbm, last_hi_ref),
+        (last_lo_hbm, last_lo_ref),
+        (mid_hi_hbm, mid_hi_ref),
+        (mid_lo_hbm, mid_lo_ref),
+        (twist_cos_hbm, twist_cos_ref),
+        (twist_sin_hbm, twist_sin_ref),
+    )
+    loads = [
+        pltpu.make_async_copy(source, target, load_sem.at[place])
+        for place, (source, target) in enumerate(held)
+    ]
+    loads.append(
+        pltpu.make_async_copy(
+            weight_ref.at[pl.ds(mine * width, width)], weight_all.at[mine], load_sem.at[len(held)]
+        )
+    )
+    for load in loads:
+        load.start()
+    for place in (0, 1, 3):
+        loads[place].wait()
 
     mixed = (signal_ref[...].astype(F32) * value_ref[...].astype(F32)).astype(BF16)
     row_id = lax.broadcasted_iota(jnp.int32, (2 * width, width), 0)
@@ -122,9 +183,9 @@
 
     pl.semaphore_wait(barrier, groups + chans - 2)
 
-    @pl.loop(1, groups)
+    @pl.loop(0, groups - 1)
     def _(step):
-        peer = lax.rem(me + step, groups)
+        peer = peer_of(step)
         pltpu.make_async_remote_copy(
             src_ref=out_bf.at[peer],
             dst_ref=in_bf.at[me],
@@ -147,7 +208,8 @@
         ).start()
 
     in_bf[pl.ds(me, 1)] = out_bf[pl.ds(me, 1)]
-    weight_all[pl.ds(mine, 1)] = weight_ref[pl.ds(mine * width, width)].reshape(1, width, width)
+    for place in (2, *range(4, len(loads))):
+        loads[place].wait()
     positions = me * rows + lax.broadcasted_iota(jnp.int32, (rows, starts_ref.shape[1]), 0)
     counted = jnp.sum(
         jnp.where(starts_ref[...] <= positions, 1.0, 0.0).astype(F32), axis=1, keepdims=True
@@ -198,9 +260,9 @@
         back_f32[:, 2 * slot + 1, :] = result[:, half:]
     back_bf[...] = back_f32[...].astype(BF16)
 
-    @pl.loop(1, groups)
+    @pl.loop(0, groups - 1)
     def _(step):
-        peer = lax.rem(me + step, groups)
+        peer = peer_of(step)
         pltpu.make_async_remote_copy(
             src_ref=back_bf.at[peer],
             dst_ref=home_bf.at[me],
@@ -226,21 +288,35 @@
         gated = (scale[span] * (conv + direct[span])).astype(BF16)
         gated_all[pl.ds(mine, 1), span, :] = gated.reshape(1, half, width)
 
-    def gated_copy(source, peer, index):
-        return pltpu.make_async_remote_copy(
-            src_ref=gated_all.at[source],
-            dst_ref=gated_all.at[source],
-            send_sem=gated_send_sem.at[index],
-            recv_sem=gated_recv_sem.at[source],
+    sends = []
+    piece = rows // PIECES
+
+    def gated_copy(source, part, peer):
+        block = gated_all.at[source, pl.ds(part * piece, piece)]
+        copy = pltpu.make_async_remote_copy(
+            src_ref=block,
+            dst_ref=block,
+            send_sem=gated_send_sem.at[len(sends)],
+            recv_sem=gated_recv_sem.at[source, part],
             device_id={"chan": peer},
             device_id_type=MESH,
         )
-
-    sources = [lax.rem(mine + 2 * step, chans) for step in range(1, chans // 2)]
-    sends = [gated_copy(mine, peer, index) for index, peer in enumerate(sources)]
-    sends.append(gated_copy(mine, sibling, len(sources)))
-    for send in sends:
-        send.start()
+        copy.start()
+        sends.append(copy)
+
+    def arrived(source, part):
+        block = gated_all.at[source, pl.ds(part * piece, piece)]
+        pltpu.make_async_copy(block, block, gated_recv_sem.at[source, part]).wait()
+
+    right, far, left = [lax.rem(mine + 2 * step, chans) for step in (1, 2, 3)]
+    via, back = left, right
+    gated_copy(mine, 1, via)
+    gated_copy(mine, 0, far)
+    gated_copy(mine, 0, via)
+    gated_copy(mine, 0, back)
+    gated_copy(mine, 1, back)
+    for part in range(PIECES):
+        gated_copy(mine, part, sibling)
 
     whole = weight_all.at[pl.ds(0, chans - 1)]
     pltpu.make_async_copy(whole, whole, weight_recv_sem).wait()
@@ -248,23 +324,22 @@
     def term(source):
         return dot(gated_all[source], weight_all[source], ((1,), (1,)))
 
-    def arrived(source):
-        block = gated_all.at[source]
-        pltpu.make_async_copy(block, block, gated_recv_sem.at[source]).wait()
-
     total = term(mine)
-    order = sorted(range(len(sources)), key=lambda i: min(i + 1, len(sources) - i))
-    for i in order:
-        arrived(sources[i])
-        forward = gated_copy(sources[i], sibling, len(sources) + 1 + i)
-        forward.start()
-        sends.append(forward)
-        total += term(sources[i])
-    arrived(sibling)
+    for part in range(PIECES):
+        arrived(sibling, part)
     total += term(sibling)
-    for i in order:
-        other = lax.rem(sources[i] + 1, 2) * 1 + (sources[i] - lax.rem(sources[i], 2))
-        arrived(other)
+    arrived(back, 1)
+    gated_copy(back, 1, via)
+    gated_copy(back, 1, sibling)
+    for source, part in ((back, 0), (via, 0), (far, 0), (via, 1), (far, 1)):
+        arrived(source, part)
+        gated_copy(source, part, sibling)
+    for source in (far, left, right):
+        total += term(source)
+    for source in (far, left, right):
+        other = source + 1 - 2 * core
+        for part in range(PIECES):
+            arrived(other, part)
         total += term(other)
     out_ref[...] = total.astype(BF16)
 
@@ -285,11 +360,20 @@
     chans = lax.axis_size("chan")
     own = width // groups
     tables = [jnp.asarray(table) for table in make_tables(groups, rows)]
+    held = (
+        signal_in,
+        value_in,
+        gate_in,
+        filter_taps,
+        skip_gain.reshape(1, width),
+        turn_starts.reshape(1, -1),
+        *tables,
+    )
     dma = pltpu.SemaphoreType.DMA
     return pl.pallas_call(
         functools.partial(kernel, groups, chans),
         out_shape=jax.ShapeDtypeStruct((rows, width), BF16),
-        in_specs=[pl.BlockSpec(memory_space=pltpu.VMEM)] * (7 + len(tables)),
+        in_specs=[pl.BlockSpec(memory_space=pl.ANY)] * (7 + len(tables)),
         out_specs=pl.BlockSpec(memory_space=pltpu.VMEM),
         scratch_shapes=[
             pltpu.VMEM((groups, 2 * own, rows), BF16),
@@ -302,26 +386,19 @@
             pltpu.VMEM((groups, 2 * own, rows // 2), BF16),
             pltpu.VMEM((chans, rows, width), BF16),
             pltpu.VMEM((chans, width, width), BF16),
-            dma,
-            dma,
-            dma,
-            dma,
-            dma,
-            dma,
-            dma((chans,)),
-            dma((chans,)),
+            *[pltpu.VMEM(array.shape, array.dtype) for array in held],
+            dma((len(held) + 1,)),
+            dma,
+            dma,
+            dma,
+            dma,
+            dma,
+            dma,
+            dma((7 * PIECES,)),
+            dma((chans, PIECES)),
         ],
         compiler_params=pltpu.CompilerParams(collective_id=0, has_side_effects=True),
-    )(
-        signal_in,
-        value_in,
-        gate_in,
-        filter_taps,
-        skip_gain.reshape(1, width),
-        turn_starts.reshape(1, -1),
-        out_weight,
-        *tables,
-    )
+    )(*held[:6], out_weight, *held[6:])
 
 
 def solution(mesh):

time: 51.3 us -> 49 us (0.955)
  Pallas kernels: 49.6 us -> 47.2 us
    pallas_call x1, Pallas kernels: 49.6 us -> 47.2 us  [on_device(): pl.pallas_call(functools.partial(kernel, groups, chans), out_shape=jax.Sh...]
where the time goes in v2:
time: 49 us; the launch traced here: 48.8 us
  Pallas kernels  47.2 us (96%)
  local copies, waits for them, and re-layouts  1.57 us (3%)
    pallas_call x1, Pallas kernels, on_device(): pl.pallas_call(functools.partial(kernel, groups, chans), out_shape=jax.Sh...  47.2 us
    unnamed x1, local copies, waits for them, and re-layouts  1.57 us

profile of v2, /device:TPU:1, one launch (start us, length us, event | category | flops | bytes accessed | tf_op | source)
XLA Modules:
  0.0 48.8 jit_solution(9767731264764959598)
XLA Ops:
  0.0 47.2 %shard_map.145 = bf16[256,256]{1,0:T(8,128)(2,1)} custom-call(bf16[256,256]{1,0:T(8,128)(2,1)} %signal_hbm.1, bf16[256,256]{1,0:T(8,128)(2,1)} %value_hbm.1, bf16[256,256]{1,0:T(8,128)(2,1)} %gate_hbm.1, bf16[256,256]{1,0:T(8,128)(2,1)} %taps_hbm.1, f32[1,256]{1,0:T(1,128)} %bitcast.2, s32[1,32]{1,0:T(1,128)} %bitcast.3, bf16[2048,256]{1,0:T(8,128)(2,1)} %weight_ref.1, ...), custom_call_target="tpu_custom_call" | custom-call | tf_op jit(solution)/shard_map/pallas_call | solution.py:373
  47.3 1.6 %copy.17 = bf16[256,256]{1,0:T(8,128)(2,1)} copy(bf16[256,256]{1,0:T(8,128)(2,1)} %shard_map.145) | data formatting | bytes 262144

commit v3 on v2

--- a/solution.py
+++ b/solution.py
@@ -53,7 +53,7 @@
 
 
 def farthest(step, size):
-    return lax.rem(size // 2 + (1 - 2 * lax.rem(step, 2)) * ((step + 1) // 2), size)
+    return (size // 2 + (1 - 2 * (step % 2)) * ((step + 1) // 2)) % size
 
 
 def kernel(
@@ -119,22 +119,24 @@
     core = lax.rem(mine, 2)
     sibling = mine + 1 - 2 * core
 
-    def along_row(step):
-        return lax.rem(col + farthest(step, side), side)
-
-    def along_col(step):
-        return lax.rem(row + farthest(step, side), side)
-
-    def peer_of(step):
-        return along_col(step // side) * side + along_row(lax.rem(step, side))
+    cols = [lax.rem(col + farthest(step, side), side) for step in range(side)]
+
+    def for_peers(act):
+        @pl.loop(0, side - 1)
+        def _(step):
+            offset = side // 2 + (1 - 2 * lax.rem(step, 2)) * ((step + 1) // 2)
+            base = lax.rem(row + offset, side) * side
+            for other in cols:
+                act(base + other)
+
+        for other in cols[:-1]:
+            act(row * side + other)
 
     barrier = pltpu.get_barrier_semaphore()
 
-    @pl.loop(0, groups - 1)
-    def _(step):
-        pl.semaphore_signal(
-            barrier, inc=1, device_id={"seq": peer_of(step)}, device_id_type=MESH
-        )
+    @for_peers
+    def _(peer):
+        pl.semaphore_signal(barrier, inc=1, device_id={"seq": peer}, device_id_type=MESH)
 
     @pl.loop(1, chans)
     def _(step):
@@ -183,9 +185,8 @@
 
     pl.semaphore_wait(barrier, groups + chans - 2)
 
-    @pl.loop(0, groups - 1)
-    def _(step):
-        peer = peer_of(step)
+    @for_peers
+    def _(peer):
         pltpu.make_async_remote_copy(
             src_ref=out_bf.at[peer],
             dst_ref=in_bf.at[me],
@@ -260,9 +261,8 @@
         back_f32[:, 2 * slot + 1, :] = result[:, half:]
     back_bf[...] = back_f32[...].astype(BF16)
 
-    @pl.loop(0, groups - 1)
-    def _(step):
-        peer = peer_of(step)
+    @for_peers
+    def _(peer):
         pltpu.make_async_remote_copy(
             src_ref=back_bf.at[peer],
             dst_ref=home_bf.at[me],

time: 49 us -> 47.6 us (0.971)
  Pallas kernels: 47.2 us -> 45.8 us
    pallas_call x1, Pallas kernels: 47.2 us -> 45.8 us  [on_device(): pl.pallas_call(functools.partial(kernel, groups, chans), out_shape=jax.Sh...]
where the time goes in v3:
time: 47.6 us; the launch traced here: 47.4 us
  Pallas kernels  45.8 us (96%)
  local copies, waits for them, and re-layouts  1.57 us (3%)
    pallas_call x1, Pallas kernels, on_device(): pl.pallas_call(functools.partial(kernel, groups, chans), out_shape=jax.Sh...  45.8 us
    unnamed x1, local copies, waits for them, and re-layouts  1.57 us

profile of v3, /device:TPU:1, one launch (start us, length us, event | category | flops | bytes accessed | tf_op | source)
XLA Modules:
  0.0 47.4 jit_solution(4195568720575886629)
XLA Ops:
  0.0 45.8 %shard_map.145 = bf16[256,256]{1,0:T(8,128)(2,1)} custom-call(bf16[256,256]{1,0:T(8,128)(2,1)} %signal_hbm.1, bf16[256,256]{1,0:T(8,128)(2,1)} %value_hbm.1, bf16[256,256]{1,0:T(8,128)(2,1)} %gate_hbm.1, bf16[256,256]{1,0:T(8,128)(2,1)} %taps_hbm.1, f32[1,256]{1,0:T(1,128)} %bitcast.2, s32[1,32]{1,0:T(1,128)} %bitcast.3, bf16[2048,256]{1,0:T(8,128)(2,1)} %weight_ref.1, ...), custom_call_target="tpu_custom_call" | custom-call | tf_op jit(solution)/shard_map/pallas_call | solution.py:373
  45.8 1.6 %copy.17 = bf16[256,256]{1,0:T(8,128)(2,1)} copy(bf16[256,256]{1,0:T(8,128)(2,1)} %shard_map.145) | data formatting | bytes 262144

commit v4 on v3

--- a/solution.py
+++ b/solution.py
@@ -121,11 +121,10 @@
 
     cols = [lax.rem(col + farthest(step, side), side) for step in range(side)]
 
+    bases = [lax.rem(row + farthest(step, side), side) * side for step in range(side - 1)]
+
     def for_peers(act):
-        @pl.loop(0, side - 1)
-        def _(step):
-            offset = side // 2 + (1 - 2 * lax.rem(step, 2)) * ((step + 1) // 2)
-            base = lax.rem(row + offset, side) * side
+        for base in bases:
             for other in cols:
                 act(base + other)
 
@@ -273,17 +272,15 @@
         ).start()
 
     home_bf[pl.ds(me, 1)] = back_bf[pl.ds(me, 1)]
+    picks = [(row_id == 2 * col_id + part).astype(F32).astype(BF16) for part in range(2)]
     direct = skip_ref[...] * mixed.astype(F32)
     scale = gate_ref[...].astype(F32) * keep
     whole = home_bf.at[pl.ds(0, groups - 1)]
     pltpu.make_async_copy(whole, whole, back_recv_sem).wait()
 
     home = home_bf[...].astype(F32).reshape(2 * width, half).astype(BF16)
-    slot_id = lax.broadcasted_iota(jnp.int32, (2 * width, width), 0)
-    chan_id = lax.broadcasted_iota(jnp.int32, (2 * width, width), 1)
     for part in range(2):
-        pick = (slot_id == 2 * chan_id + part).astype(F32).astype(BF16)
-        conv = dot(home, pick, ((0,), (0,)))
+        conv = dot(home, picks[part], ((0,), (0,)))
         span = slice(part * half, (part + 1) * half)
         gated = (scale[span] * (conv + direct[span])).astype(BF16)
         gated_all[pl.ds(mine, 1), span, :] = gated.reshape(1, half, width)

time: 47.6 us -> 47.5 us (level)
  no operation moved by 1% of the time
where the time goes in v4:
time: 47.5 us; the launch traced here: 47.3 us
  Pallas kernels  45.8 us (96%)
  local copies, waits for them, and re-layouts  1.57 us (3%)
    pallas_call x1, Pallas kernels, on_device(): pl.pallas_call(functools.partial(kernel, groups, chans), out_shape=jax.Sh...  45.8 us
    unnamed x1, local copies, waits for them, and re-layouts  1.57 us

profile of v4, /device:TPU:1, one launch (start us, length us, event | category | flops | bytes accessed | tf_op | source)
XLA Modules:
  0.0 47.3 jit_solution(16571442704541609384)
XLA Ops:
  0.0 45.8 %shard_map.145 = bf16[256,256]{1,0:T(8,128)(2,1)} custom-call(bf16[256,256]{1,0:T(8,128)(2,1)} %signal_hbm.1, bf16[256,256]{1,0:T(8,128)(2,1)} %value_hbm.1, bf16[256,256]{1,0:T(8,128)(2,1)} %gate_hbm.1, bf16[256,256]{1,0:T(8,128)(2,1)} %taps_hbm.1, f32[1,256]{1,0:T(1,128)} %bitcast.2, s32[1,32]{1,0:T(1,128)} %bitcast.3, bf16[2048,256]{1,0:T(8,128)(2,1)} %weight_ref.1, ...), custom_call_target="tpu_custom_call" | custom-call | tf_op jit(solution)/shard_map/pallas_call | solution.py:370
  45.8 1.6 %copy.17 = bf16[256,256]{1,0:T(8,128)(2,1)} copy(bf16[256,256]{1,0:T(8,128)(2,1)} %shard_map.145) | data formatting | bytes 262144
